TPU v7x, 32 devices: a whole 2x2x4 slice. The times are simulated.
32 devices in a mesh: dp: 8 (over z, y), tensor: 4 (over x, core).
Axes of the slice: x: 2, y: 2, z: 4, core: 2. Of those that a mesh axis runs over, the one named last changes fastest.
Arguments:
- patches: bfloat16 [4096, 1280], P(('dp', 'tensor')), may hold values from -12 to 12
- ln_gain: float32 [1280], replicated, may hold values from 0.5 to 1.5
- ln_bias: float32 [1280], replicated, may hold values from -1.8 to 1.8
- fc1_weight: bfloat16 [5120, 2560], P(None, 'tensor'), may hold values from -0.078125 to 0.078125
- fc1_bias: float32 [2560], P('tensor'), may hold values from -3 to 3
- fc2_weight: bfloat16 [2560, 8192], P('tensor'), may hold values from -0.125 to 0.125
- fc2_bias: float32 [8192], replicated, may hold values from -3 to 3
- image_counts: int32 [32, 4], P(('dp', 'tensor')), may hold values from 0 to 32, as said below
- image_positions: int32 [1024], P(('dp', 'tensor')), may hold values from 0 to 4095, as said below
- text_embeds: bfloat16 [4096, 8192], P(('dp', 'tensor')), may hold values from -6 to 6
- keep_mask: int32 [4096, 8192], P(('dp', 'tensor')), may hold values 0 or 1
- norm_gain: float32 [8192], replicated, may hold values from 0.25 to 1.75
- qkv_weight: bfloat16 [8192, 10240], P('dp', 'tensor'), may hold values from -0.0625 to 0.0625
- qkv_bias: float32 [10240], P('tensor'), may hold values from -3 to 3
Outputs:
- stream: bfloat16 [4096, 8192], P(('dp', 'tensor'))
- queries: bfloat16 [4096, 8192], P('dp', 'tensor')
- keys: bfloat16 [4096, 1024], P('dp', 'tensor')
- values: bfloat16 [4096, 1024], P('dp', 'tensor')
Inputs may be any that keep to these rules, and one draw needn't show every extreme that they name: `image_counts`: A multiple of 4. In a shard, the images after its first empty one are empty. The counts of one shard sum to at most 128, which one shard reaches in every draw. `image_positions`: all slots name distinct positions. Position p lies on the device of index p // 128 of dp+tensor. The slots of a shard name positions only on devices with the shard's tensor index, exactly 4 on each of them, so every such device receives 4 slots from each shard.
All inputs are finite; a program needn't handle non-finite values. No bound on the sum of `keep_mask` on one device may be relied on, other than what follows from the above.
Results may differ from a plain program's by a relative error of at most 0.0075.
Values may be sent and summed in bfloat16 or wider, within the bound.
A program may use at most 128 MiB of HBM per device.

v0:
```python
import jax
import jax.numpy as jnp
from jax import lax
from jax.sharding import PartitionSpec as P

HEADS = 64
KV_HEADS = 8
HEAD_DIM = 128


KEEP_SCALE = 1.0 / 0.9


def layer_norm(inputs, gain, bias):
    widened = inputs.astype(jnp.float32)
    center = jnp.mean(widened, axis=-1, keepdims=True)
    spread = jnp.mean((widened - center) * (widened - center), axis=-1, keepdims=True)
    return (widened - center) * lax.rsqrt(spread + 1e-06) * gain + bias


def rms_norm(inputs, gain):
    widened = inputs.astype(jnp.float32)
    inverse = lax.rsqrt(jnp.mean(widened * widened, axis=-1, keepdims=True) + 1e-06)
    return (widened * inverse * gain).astype(jnp.bfloat16)


def merger(rows_in, fc1_weight, fc1_bias, fc2_weight, fc2_bias):
    product = (
        jnp.dot(
            lax.all_gather(rows_in, "tensor", axis=0, tiled=True),
            fc1_weight,
            preferred_element_type=jnp.float32,
        )
        + fc1_bias
    )
    hidden = jax.nn.gelu(product, approximate=False).astype(jnp.bfloat16)
    summed = lax.psum_scatter(
        jnp.dot(hidden, fc2_weight, preferred_element_type=jnp.float32).astype(jnp.bfloat16),
        "tensor",
        scatter_dimension=0,
        tiled=True,
    ).astype(jnp.float32)
    return (summed + fc2_bias).astype(jnp.bfloat16)


def route_plan(image_counts, image_positions, rows_here, groups, tensor_devs):
    slot_total = image_positions.shape[0]
    per_peer = slot_total // groups
    live_slots = jnp.sum(image_counts) // 4
    usable = jnp.arange(slot_total, dtype=jnp.int32) < live_slots
    owner_dev = image_positions // rows_here
    owner_group = owner_dev // tensor_devs
    owner_row = jnp.where(usable, image_positions % rows_here, -1)
    member = (owner_group[:, None] == jnp.arange(groups, dtype=jnp.int32)[None, :]).astype(
        jnp.int32
    )
    slot_rank = jnp.sum(member * (jnp.cumsum(member, axis=0) - 1), axis=1)
    out_slot = owner_group * per_peer + slot_rank
    chooser = out_slot[None, :] == jnp.arange(slot_total, dtype=jnp.int32)[:, None]
    send_rows = jnp.sum(jnp.where(chooser, owner_row[None, :], 0), axis=1)
    return (chooser.astype(jnp.bfloat16), send_rows.reshape(groups, per_peer))


def arrange(payload, chooser, groups):
    ordered = jnp.dot(chooser, payload, preferred_element_type=jnp.float32).astype(jnp.bfloat16)
    return ordered.reshape(groups, payload.shape[0] // groups, payload.shape[1])


def land(arrived, arrived_rows, text_rows):
    landing = arrived_rows[None, :] == jnp.arange(text_rows.shape[0], dtype=jnp.int32)[:, None]
    covered = jnp.any(landing, axis=1)
    placed = jnp.dot(
        landing.astype(jnp.bfloat16), arrived, preferred_element_type=jnp.float32
    ).astype(jnp.bfloat16)
    return jnp.where(covered[:, None], placed, text_rows)


def shards(
    patches,
    ln_gain,
    ln_bias,
    fc1_weight,
    fc1_bias,
    fc2_weight,
    fc2_bias,
    image_counts,
    image_positions,
    text_embeds,
    keep_mask,
    norm_gain,
    qkv_weight,
    qkv_bias,
):
    groups = lax.axis_size("dp")
    rows_here = text_embeds.shape[0]
    patch_normed = layer_norm(patches, ln_gain, ln_bias).astype(jnp.bfloat16)
    merged_in = patch_normed.reshape(-1, 4 * patches.shape[1])
    chooser, send_rows = route_plan(
        image_counts, image_positions, rows_here, groups, lax.axis_size("tensor")
    )
    merged_tokens = merger(merged_in, fc1_weight, fc1_bias, fc2_weight, fc2_bias)
    outgoing = arrange(merged_tokens, chooser, groups)
    arrived, arrived_rows = (
        lax.all_to_all(outgoing, "dp", split_axis=0, concat_axis=0, tiled=True),
        lax.all_to_all(send_rows, "dp", split_axis=0, concat_axis=0, tiled=True),
    )
    images = arrived.reshape(-1, arrived.shape[-1])
    placed = land(images, arrived_rows.reshape(-1), text_embeds)
    stream = (placed.astype(jnp.float32) * keep_mask.astype(jnp.float32) * KEEP_SCALE).astype(
        jnp.bfloat16
    )
    gathered = lax.all_gather(stream, "tensor", axis=0, tiled=True)
    normed = rms_norm(gathered, norm_gain)
    projected = (
        jnp.dot(
            normed,
            lax.all_gather(qkv_weight, "dp", axis=0, tiled=True),
            preferred_element_type=jnp.float32,
        )
        + qkv_bias
    )
    group_width = (HEADS // KV_HEADS + 2) * HEAD_DIM
    grouped = projected.reshape(normed.shape[0], -1, group_width)
    query_width = HEADS // KV_HEADS * HEAD_DIM
    queries = grouped[:, :, :query_width].reshape(normed.shape[0], -1).astype(jnp.bfloat16)
    keys = (
        grouped[:, :, query_width : query_width + HEAD_DIM]
        .reshape(normed.shape[0], -1)
        .astype(jnp.bfloat16)
    )
    values = (
        grouped[:, :, query_width + HEAD_DIM :].reshape(normed.shape[0], -1).astype(jnp.bfloat16)
    )
    return (stream, queries, keys, values)


def solution(mesh):
    placed = (
        P(("dp", "tensor"), None),
        P(),
        P(),
        P(None, "tensor"),
        P("tensor"),
        P("tensor", None),
        P(),
        P(("dp", "tensor"), None),
        P(("dp", "tensor")),
        P(("dp", "tensor"), None),
        P(("dp", "tensor"), None),
        P(),
        P("dp", "tensor"),
        P("tensor"),
    )
    return jax.shard_map(
        shards,
        mesh=mesh,
        in_specs=placed,
        out_specs=(
            P(("dp", "tensor"), None),
            P("dp", "tensor"),
            P("dp", "tensor"),
            P("dp", "tensor"),
        ),
        check_vma=False,
    )
```

profile of v0, /device:TPU:0, one launch (start us, length us, event | category | flops | bytes accessed | tf_op | source)
XLA Modules:
  0.0 1001.3 jit_solution(17281969107623745771)
XLA Ops:
  7.2 1.1 convert_reduce_fusion
  8.3 1.2 fusion.16
  9.5 1.3 fusion.19
  10.8 0.9 reshape.62
  11.8 21.0 %all-gather.4.cloned.1.call-done = bf16[128,5120]{1,0:T(8,128)(2,1)} async-done(((bf16[32,5120]{1,0:T(8,128)(2,1)}), bf16[128,5120]{1,0:T(8,128)(2,1)}) %all-gather.4.cloned.1.call-update) | async-done | bytes 1310736 | tf_op jit(solution)/shard_map/all_gather | solution.py:30
  32.8 11.2 %convolution_convert_fusion.1 = bf16[128,8192]{1,0:T(8,128)(2,1)} fusion(bf16[640,8192]{1,0:T(8,128)(2,1)} %param.19, bf16[128,5120]{1,0:T(8,128)(2,1)} %all-gather.4.cloned.1.call-done, bf16[5120,640]{1,0:T(8,128)(2,1)} %param.17, f32[640]{0:T(1024)} %param.18), kind=kOutput, calls=%fused_computation.6 | convolution fusion | flops 2187493376 | bytes 20449792 | tf_op jit(solution)/shard_map/dot_general | solution.py:38
  44.0 0.6 reduce_sum.55
  47.7 0.7 all_to_all.9
  48.4 5.5 all-to-all-start
  53.9 21.4 %reduce-scatter.2.cloned.1.call-done = bf16[32,8192]{1,0:T(8,128)(2,1)} async-done(((bf16[128,8192]{1,0:T(8,128)(2,1)}), bf16[32,8192]{1,0:T(8,128)(2,1)}) %reduce-scatter.2.cloned.1.call-update) | async-done | bytes 524304 | tf_op jit(solution)/shard_map/reduce_scatter | solution.py:37
  75.3 1.3 convolution_convert_fusion.2
  76.6 1.0 reshape.63
  77.6 5.5 all-to-all-start.1
  83.7 0.7 reduce.3
  84.6 12.9 %all-to-all-done.1 = bf16[8,4,8192]{2,1,0:T(4,128)(2,1)S(1)} async-done(((bf16[8,4,8192]{2,1,0:T(4,128)(2,1)}), bf16[8,4,8192]{2,1,0:T(4,128)(2,1)S(1)}, u32[]{:S(2)}, u32[]{:S(2)}) %all-to-all-start.1) | async-done | bytes 524320 | tf_op jit(solution)/shard_map/all_to_all | solution.py:104
  97.6 4.7 fusion.7
  102.9 55.9 %all-gather.6.cloned.1.call-done = bf16[512,8192]{1,0:T(8,128)(2,1)} async-done(((bf16[128,8192]{1,0:T(8,128)(2,1)}), bf16[512,8192]{1,0:T(8,128)(2,1)}) %all-gather.6.cloned.1.call-update) | async-done | bytes 8388624 | tf_op jit(solution)/shard_map/all_gather | solution.py:112
  158.8 5.1 fusion
  164.0 791.3 %all-gather.8.cloned.1.call-done = bf16[8192,2560]{1,0:T(8,128)(2,1)} async-done(((bf16[1024,2560]{1,0:T(8,128)(2,1)}), bf16[8192,2560]{1,0:T(8,128)(2,1)}) %all-gather.8.cloned.1.call-update) | async-done | bytes 41943056 | tf_op jit(solution)/shard_map/all_gather | solution.py:117
  955.2 29.4 %add_convert_fusion = bf16[512,2560]{1,0:T(8,128)(2,1)} fusion(bf16[8192,2560]{1,0:T(8,128)(2,1)} %all-gather.8.cloned.1.call-done, bf16[512,8192]{1,0:T(8,128)(2,1)} %all-gather.6.cloned.1.call-done, f32[8192]{0:T(1024)S(1)} %copy-done.3, f32[512]{0:T(512)S(1)} %add_rsqrt_fusion, f32[2560]{0:T(1024)S(1)} %copy-done.4), kind=kOutput, calls=%fused_computation.16 | convolution fusion | flops 21494235136 | bytes 52998144 | tf_op jit(solution)/shard_map/dot_general | solution.py:115
  984.6 5.5 reshape.66
  990.5 1.4 slice.15
  991.9 1.9 copy.20
  993.9 0.9 copy_bitcast_fusion
  (35 shorter events, 2.4 us)
Async XLA Ops:
  7.2 25.6 %all-gather.4.cloned.1.call-start = ((), (), s32[]{:S(2)}) async-start(), calls=%async_computation.3 | async-start | bytes 1638400 | tf_op jit(solution)/shard_map/all_gather | solution.py:30
  11.8 32.2 %copy-start.5 = (s32[1,4]{1,0:T(1,128)S(1)}, s32[1,4]{1,0:T(1,128)}, u32[]{:S(2)}) copy-start(s32[1,4]{1,0:T(1,128)} %param.21) | copy-start | bytes 52
  11.8 35.5 %copy-start.2 = (s32[32]{0:T(128)S(1)}, s32[32]{0:T(128)}, u32[]{:S(2)}) copy-start(s32[32]{0:T(128)} %param.22) | copy-start | bytes 388
  11.8 63.5 %copy-start.1 = (f32[8192]{0:T(1024)S(1)}, f32[8192]{0:T(1024)}, u32[]{:S(2)}) copy-start(f32[8192]{0:T(1024)} %param.20) | copy-start | bytes 98308
  11.8 63.5 %reduce-scatter.2.cloned.1.call-start = ((), (), s32[]{:S(2)}) async-start(), calls=%async_computation.4 | async-start | bytes 2621440 | tf_op jit(solution)/shard_map/reduce_scatter | solution.py:37
  44.0 53.6 %copy-start = (bf16[128,8192]{1,0:T(8,128)(2,1)S(1)}, bf16[128,8192]{1,0:T(8,128)(2,1)}, u32[]{:S(2)}) copy-start(bf16[128,8192]{1,0:T(8,128)(2,1)} %param.23) | copy-start | bytes 6291460
  48.4 29.3 %all-to-all-start = ((s32[8,1,4]{2,1,0:T(1,128)}), s32[8,1,4]{2,1,0:T(1,128)S(1)}, u32[]{:S(2)}, u32[]{:S(2)}) async-start(s32[8,1,4]{2,1,0:T(1,128)} %bitcast), calls=%async_computation | async-start | bytes 8192 | tf_op jit(solution)/shard_map/all_to_all | solution.py:105
  77.6 19.8 %all-to-all-start.1 = ((bf16[8,4,8192]{2,1,0:T(4,128)(2,1)}), bf16[8,4,8192]{2,1,0:T(4,128)(2,1)S(1)}, u32[]{:S(2)}, u32[]{:S(2)}) async-start(bf16[8,4,8192]{2,1,0:T(4,128)(2,1)} %reshape.63), calls=%async_computation.2 | async-start | bytes 1048576 | tf_op jit(solution)/shard_map/all_to_all | solution.py:104
  83.2 75.7 %all-gather.6.cloned.1.call-start = ((), (), s32[]{:S(2)}) async-start(), calls=%async_computation.5 | async-start | bytes 10485760 | tf_op jit(solution)/shard_map/all_gather | solution.py:112
  102.3 852.9 %all-gather.8.cloned.1.call-start = ((), (), s32[]{:S(2)}) async-start(), calls=%async_computation.6 | async-start | bytes 47185920 | tf_op jit(solution)/shard_map/all_gather | solution.py:117
  102.9 852.3 %copy-start.3 = (f32[8192]{0:T(1024)S(1)}, f32[8192]{0:T(1024)}, u32[]{:S(2)}) copy-start(f32[8192]{0:T(1024)} %param.25) | copy-start | bytes 98308
  102.9 852.3 %copy-start.4 = (f32[2560]{0:T(1024)S(1)}, f32[2560]{0:T(1024)}, u32[]{:S(2)}) copy-start(f32[2560]{0:T(1024)} %param.27) | copy-start | bytes 30724
Sparse Core Ops, SparseCore 0:
  11.9 20.8 all-gather.3
  44.1 31.1 reduce-scatter.1
  102.4 56.3 all-gather.5
  160.2 794.9 all-gather.7
where the time goes:
time: 1000 us
  waiting for transfers between devices  903 us (90%)
  matrix products  46.5 us (5%)
  between operations  16.5 us (2%)
  local copies, waits for them, and re-layouts  13.4 us (1%)
  starting transfers between devices  11.4 us (1%)
  other arithmetic  10.5 us (1%)
    all_gather x1, waiting for transfers between devices, shards(): lax.all_gather(qkv_weight, 'dp', axis=0, tiled=True)  791 us
    all_gather x1, waiting for transfers between devices, shards(): gathered = lax.all_gather(stream, 'tensor', axis=0, tiled=True)  55.9 us
    dot_general x1, matrix products, shards(): jnp.dot(normed, lax.all_gather(qkv_weight, 'dp', axis=0, tiled=True), pre...  29.4 us
    reduce_scatter x1, waiting for transfers between devices, merger(): lax.psum_scatter(jnp.dot(hidden, fc2_weight, preferred_element_type=jnp.f...  21.4 us
    all_gather x1, waiting for transfers between devices, merger(): lax.all_gather(rows_in, 'tensor', axis=0, tiled=True)  21 us
  transfers between devices with their start and end apart: 6, of which 5 were waited for; matrix products, arithmetic and copies ran while one was open for 1% of the time, Pallas kernels for 0%

commit v1 on v0

v1 whole, which is shorter than its diff:
```python
import functools

import jax
import jax.numpy as jnp
from jax import lax
from jax.experimental import pallas as pl
from jax.experimental.pallas import tpu as pltpu
from jax.sharding import PartitionSpec as P


HEADS = 64
KV_HEADS = 8
HEAD_DIM = 128

CHUNKS = 4

KEEP_SCALE = 1.0 / 0.9


def layer_norm(inputs, gain, bias):
    widened = inputs.astype(jnp.float32)
    center = jnp.mean(widened, axis=-1, keepdims=True)
    spread = jnp.mean((widened - center) * (widened - center), axis=-1, keepdims=True)
    return (widened - center) * lax.rsqrt(spread + 1e-06) * gain + bias


def rms_norm(inputs, gain):
    widened = inputs.astype(jnp.float32)
    inverse = lax.rsqrt(jnp.mean(widened * widened, axis=-1, keepdims=True) + 1e-06)
    return (widened * inverse * gain).astype(jnp.bfloat16)


def swap(block, axis, bits):
    return lax.ppermute(block, axis, [(i, i ^ bits) for i in range(lax.axis_size(axis))])


def merger(rows_in, fc1_weight, fc1_bias, fc2_weight, fc2_bias):
    peers = lax.axis_size("tensor")
    rows = rows_in.shape[0]
    gathered = jnp.concatenate([rows_in] + [swap(rows_in, "tensor", k) for k in range(1, peers)])
    product = jnp.dot(gathered, fc1_weight, preferred_element_type=jnp.float32) + fc1_bias
    hidden = jax.nn.gelu(product, approximate=False).astype(jnp.bfloat16)
    terms = jnp.dot(hidden, fc2_weight, preferred_element_type=jnp.float32).astype(jnp.bfloat16)
    summed = terms[:rows].astype(jnp.float32)
    for k in range(1, peers):
        arrived = swap(terms[k * rows : (k + 1) * rows], "tensor", k)
        summed = summed + arrived.astype(jnp.float32)
    return (summed + fc2_bias).astype(jnp.bfloat16)


def after(value, earlier):
    return lax.optimization_barrier((value, earlier))[0]


def route_plan(image_counts, image_positions, rows_here, groups, tensor_devs):
    slot_total = image_positions.shape[0]
    per_peer = slot_total // groups
    live_slots = jnp.sum(image_counts) // 4
    usable = jnp.arange(slot_total, dtype=jnp.int32) < live_slots
    owner_dev = image_positions // rows_here
    owner_group = owner_dev // tensor_devs
    owner_row = jnp.where(usable, image_positions % rows_here, -1)
    member = (owner_group[:, None] == jnp.arange(groups, dtype=jnp.int32)[None, :]).astype(
        jnp.int32
    )
    slot_rank = jnp.sum(member * (jnp.cumsum(member, axis=0) - 1), axis=1)
    out_slot = owner_group * per_peer + slot_rank
    chooser = out_slot[None, :] == jnp.arange(slot_total, dtype=jnp.int32)[:, None]
    landing = owner_row[:, None] == jnp.arange(rows_here, dtype=jnp.int32)[None, :]
    return chooser.astype(jnp.bfloat16), landing.astype(jnp.bfloat16)


def arrange(payload, chooser, groups):
    ordered = jnp.dot(chooser, payload, preferred_element_type=jnp.float32).astype(jnp.bfloat16)
    return ordered.reshape(groups, payload.shape[0] // groups, payload.shape[1])


def scatter_rows(landing, rows):
    return lax.dot_general(
        landing, rows, (((0,), (0,)), ((), ())), preferred_element_type=jnp.float32
    )


def keep_rows(rows, keep):
    return (rows.astype(jnp.float32) * keep * KEEP_SCALE).astype(jnp.bfloat16)


def chunk_bounds(columns):
    tile = 2 * HEAD_DIM
    tiles = columns // tile
    chunks = min(CHUNKS, tiles)
    sizes = [tiles // chunks + (c < tiles % chunks) for c in range(chunks)]
    starts = [sum(sizes[:c]) * tile for c in range(chunks)]
    return [(start, start + size * tile) for start, size in zip(starts, sizes)]


def assemble_kernel(blocks, place, *refs):
    text_refs = refs[:blocks]
    image_refs = refs[blocks : 2 * blocks]
    landing_refs = refs[2 * blocks : 3 * blocks]
    out_ref = refs[-1]
    rows = text_refs[0].shape[0]
    for k in range(blocks):
        landing = landing_refs[k][...]
        moved = scatter_rows(landing, image_refs[k][...]).astype(out_ref.dtype)
        hits = scatter_rows(landing, jnp.ones(landing.shape, landing.dtype))[:, :1]
        at = pl.multiple_of(lax.bitwise_xor(place[0], k) * rows, rows)
        out_ref[pl.ds(at, rows), :] = jnp.where(hits > 0.5, moved, text_refs[k][...])


def assemble(text_blocks, image_blocks, place):
    blocks = len(text_blocks)
    rows, deep = text_blocks[0].shape
    slots, _ = image_blocks[0].shape
    tile = deep // 4
    return pl.pallas_call(
        functools.partial(assemble_kernel, blocks),
        grid_spec=pltpu.PrefetchScalarGridSpec(
            num_scalar_prefetch=1,
            grid=(deep // tile,),
            in_specs=[pl.BlockSpec((rows, tile), lambda i, place: (0, i))] * blocks
            + [pl.BlockSpec((slots, tile), lambda i, place: (0, i))] * blocks
            + [pl.BlockSpec((slots, rows), lambda i, place: (0, deep // rows))] * blocks,
            out_specs=pl.BlockSpec((blocks * rows, tile), lambda i, place: (0, i)),
        ),
        out_shape=jax.ShapeDtypeStruct((blocks * rows, deep), jnp.bfloat16),
        cost_estimate=pl.CostEstimate(
            flops=0, bytes_accessed=4 * blocks * rows * deep, transcendentals=0
        ),
        name="assemble",
    )(place, *text_blocks, *image_blocks, *image_blocks)


def start_weights(chunk, half):
    return [chunk] + [swap(chunk, "dp", k) for k in (range(1, half) if half != 4 else (1, 2))]


def relay_weights(blocks, half, forward_over, ready):
    if half != 4:
        return blocks
    relayed = blocks[1] if forward_over == 2 else blocks[2]
    return blocks + [swap(after(relayed, ready), "dp", forward_over)]


def spread_rows(rows_here):
    held = {0: rows_here}
    bits = lax.axis_size("tensor") // 2
    while bits:
        held.update({k | bits: swap(block, "tensor", bits) for k, block in list(held.items())})
        bits //= 2
    return [held[k] for k in range(len(held))]


def half_product_kernel(tokens, *refs):
    weight_refs, out_ref = refs[:-1], refs[-1]
    total = None
    for k, weight_ref in enumerate(weight_refs):
        deep = weight_ref.shape[0]
        term = jnp.dot(
            tokens[:, k * deep : (k + 1) * deep],
            weight_ref[...],
            preferred_element_type=jnp.float32,
        )
        total = term if total is None else total + term
    out_ref[...] = total.astype(out_ref.dtype)


def half_product(tokens, pieces, held_as):
    tile = 2 * HEAD_DIM
    rows, deep = tokens.shape
    width = pieces[0].shape[1]
    return pl.pallas_call(
        half_product_kernel,
        grid=(width // tile,),
        in_specs=[pl.BlockSpec((rows, deep), lambda i: (0, 0))]
        + [pl.BlockSpec((block.shape[0], tile), lambda i: (0, i)) for block in pieces],
        out_specs=pl.BlockSpec((rows, tile), lambda i: (0, i)),
        out_shape=jax.ShapeDtypeStruct((rows, width), held_as),
        cost_estimate=pl.CostEstimate(
            flops=2 * rows * deep * width,
            bytes_accessed=2 * deep * (width + rows),
            transcendentals=0,
        ),
        compiler_params=pltpu.CompilerParams(vmem_limit_bytes=48 * 1024 * 1024),
    )(tokens, *pieces)


def finish_kernel(bounds, tiles, bias_ref, *refs):
    chunks = len(bounds)
    here_refs, there_refs = refs[:chunks], refs[chunks : 2 * chunks]
    queries, keys, values = refs[2 * chunks :]
    step = pl.program_id(0)
    for (first, last), here_ref, there_ref in zip(bounds, here_refs, there_refs):

        @pl.when((step >= first) & (step < last))
        def _():
            result = here_ref[...] + there_ref[...].astype(jnp.float32) + bias_ref[...]
            rounded = result.astype(jnp.bfloat16)

            @pl.when(step % tiles < tiles - 1)
            def _():
                queries[...] = rounded

            @pl.when(step % tiles == tiles - 1)
            def _():
                keys[...] = rounded[:, :HEAD_DIM]
                values[...] = rounded[:, HEAD_DIM:]


def finish(here, there, bias):
    tile = 2 * HEAD_DIM
    rows = here[0].shape[0]
    width = bias.shape[0]
    tiles = (HEADS // KV_HEADS + 2) * HEAD_DIM // tile
    groups = width // tile // tiles
    bounds = [(a // tile, b // tile) for a, b in chunk_bounds(width)]

    def chunk_map(first, last):
        return lambda i: (0, jnp.clip(i - first, 0, last - first - 1))

    return pl.pallas_call(
        functools.partial(finish_kernel, bounds, tiles),
        grid=(width // tile,),
        in_specs=[pl.BlockSpec((1, tile), lambda i: (0, i))]
        + [pl.BlockSpec((rows, tile), chunk_map(*edges)) for edges in bounds + bounds],
        out_specs=[
            pl.BlockSpec(
                (rows, tile),
                lambda i: (0, i // tiles * (tiles - 1) + jnp.minimum(i % tiles, tiles - 2)),
            ),
            pl.BlockSpec((rows, HEAD_DIM), lambda i: (0, i // tiles)),
            pl.BlockSpec((rows, HEAD_DIM), lambda i: (0, i // tiles)),
        ],
        out_shape=[
            jax.ShapeDtypeStruct((rows, groups * (tiles - 1) * tile), jnp.bfloat16),
            jax.ShapeDtypeStruct((rows, groups * HEAD_DIM), jnp.bfloat16),
            jax.ShapeDtypeStruct((rows, groups * HEAD_DIM), jnp.bfloat16),
        ],
        name="finish",
    )(bias[None, :], *here, *there)


def k_order(rows, half, deep, extra):
    here = lax.axis_index("dp")
    within, mine = here % half, here // half
    return [
        jnp.concatenate(
            [
                lax.dynamic_slice_in_dim(
                    rows,
                    (side * half + lax.bitwise_xor(within, jnp.int32(k))) * deep,
                    deep,
                    axis=1,
                )
                for k in range(half)
            ]
            + extra,
            axis=1,
        )
        for side in (mine, 1 - mine)
    ]


def shards(
    patches,
    ln_gain,
    ln_bias,
    fc1_weight,
    fc1_bias,
    fc2_weight,
    fc2_bias,
    image_counts,
    image_positions,
    text_embeds,
    keep_mask,
    norm_gain,
    qkv_weight,
    qkv_bias,
):
    groups = lax.axis_size("dp")
    rows_here, width = text_embeds.shape
    half = groups // 2
    deep = qkv_weight.shape[0]
    patch_normed = layer_norm(patches, ln_gain, ln_bias).astype(jnp.bfloat16)
    merged_in = patch_normed.reshape(-1, 4 * patches.shape[1])
    chooser, landing = route_plan(
        image_counts, image_positions, rows_here, groups, lax.axis_size("tensor")
    )
    keep = keep_mask.astype(jnp.float32)
    text_stream = keep_rows(text_embeds, keep)
    text_own, text_sent = k_order(rms_norm(text_stream, norm_gain), half, deep, [])
    text_there = swap(text_sent, "dp", half)

    merged_tokens = merger(merged_in, fc1_weight, fc1_bias, fc2_weight, fc2_bias)
    outgoing = arrange(jnp.concatenate([merged_tokens, landing], axis=1), chooser, groups)
    arrived = lax.all_to_all(outgoing, "dp", split_axis=0, concat_axis=0, tiled=True)
    arrived = arrived.reshape(-1, arrived.shape[-1])
    images, landed = arrived[:, :width], arrived[:, width:]
    image_keep = jnp.dot(
        landed, keep_mask.astype(jnp.bfloat16), preferred_element_type=jnp.float32
    )
    image_stream = keep_rows(images, image_keep)
    image_own, image_sent = k_order(rms_norm(image_stream, norm_gain), half, deep, [landed])
    image_there = swap(image_sent, "dp", half)
    image_there = spread_rows(image_there)
    image_own = spread_rows(image_own)
    covered = jnp.sum(landed.astype(jnp.float32), axis=0) > 0.5
    stream = jnp.where(
        covered[:, None], scatter_rows(landed, image_stream).astype(jnp.bfloat16), text_stream
    )

    blocks = []
    for c, (first, last) in enumerate(chunk_bounds(qkv_weight.shape[1])):
        chunk = qkv_weight[:, first:last]
        blocks.append(start_weights(chunk if c < 2 else after(chunk, outgoing), half))

    place = lax.axis_index("tensor")[None]
    tokens_there = assemble(spread_rows(text_there), image_there, place)
    text_own = spread_rows(after(text_own, outgoing))
    ready = [outgoing, image_sent]
    there, here = [], []
    for c in range(len(blocks)):
        over = 2 if c == 1 else 1
        pieces = relay_weights(blocks[c], half, over, ready[c])
        partial = half_product(tokens_there, pieces, jnp.bfloat16)
        ready.append(partial)
        there.append(swap(partial, "dp", half))
        blocks[c] = pieces
        if c == 1:
            tokens_own = assemble([after(text_own[0], partial)] + text_own[1:], image_own, place)
        if c >= 1:
            for own in range(0 if c == 1 else c, c + 1):
                tokens_own = after(tokens_own, partial)
                here.append(half_product(tokens_own, blocks[own], jnp.float32))
            tokens_there = after(tokens_there, here[-1])
    queries, keys, values = finish(here, there, qkv_bias)
    return (stream, queries, keys, values)


def solution(mesh):
    placed = (
        P(("dp", "tensor"), None),
        P(),
        P(),
        P(None, "tensor"),
        P("tensor"),
        P("tensor", None),
        P(),
        P(("dp", "tensor"), None),
        P(("dp", "tensor")),
        P(("dp", "tensor"), None),
        P(("dp", "tensor"), None),
        P(),
        P("dp", "tensor"),
        P("tensor"),
    )
    return jax.shard_map(
        shards,
        mesh=mesh,
        in_specs=placed,
        out_specs=(
            P(("dp", "tensor"), None),
            P("dp", "tensor"),
            P("dp", "tensor"),
            P("dp", "tensor"),
        ),
        check_vma=False,
    )
```

time: 1000 us -> 362 us (0.36)
  waiting for transfers between devices: 903 us -> 201 us
  Pallas kernels: 0 us -> 72.1 us
  matrix products: 46.5 us -> 15.8 us
  starting transfers between devices: 11.4 us -> 36.3 us
  between operations: 16.5 us -> 4.12 us
    all_gather x3 -> x0, waiting for transfers between devices: 868 us -> none  [the longest x1 791 us: shards(): lax.all_gather(qkv_weight, 'dp', axis=0, tiled=True)]
    ppermute x0 -> x36, waiting for transfers between devices: none -> 200 us  [swap(): lax.ppermute(block, axis, [(i, i ^ bits) for i in range(lax.axis_size(axi...]
    pallas_call x0 -> x11, Pallas kernels: none -> 72.1 us  [the longest x8 51 us: half_product(): pl.pallas_call(half_product_kernel, grid=(width // tile,), in_specs=[pl.B...]
    ppermute x0 -> x36, starting transfers between devices: none -> 31.4 us  [swap(): lax.ppermute(block, axis, [(i, i ^ bits) for i in range(lax.axis_size(axi...]
    dot_general x2, matrix products: 34.1 us -> 5.74 us  [the longest x1 2.99 us: shards(): jnp.dot(landed, keep_mask.astype(jnp.bfloat16), preferred_element_type=jn...]
    reduce_scatter x1 -> x0, waiting for transfers between devices: 21.4 us -> none  [merger(): lax.psum_scatter(jnp.dot(hidden, fc2_weight, preferred_element_type=jnp.f...]
    all_to_all x1, waiting for transfers between devices: 12.9 us -> 0.99 us  [shards(): lax.all_to_all(outgoing, 'dp', split_axis=0, concat_axis=0, tiled=True)]
  transfers between devices with their start and end apart: 6 -> 37, of which waited for: 5 -> 15; matrix products, arithmetic and copies ran while one was open for 1% -> 10% of each run, Pallas kernels for 0% -> 17%
where the time goes in v1:
time: 362 us; the launch traced here: 361 us
  waiting for transfers between devices  201 us (56%)
  Pallas kernels  72.1 us (20%)
  starting transfers between devices  36.3 us (10%)
  local copies, waits for them, and re-layouts  18.4 us (5%)
  matrix products  15.8 us (4%)
  other arithmetic  13.7 us (4%)
  between operations  4.12 us (1%)
    ppermute x36, waiting for transfers between devices, swap(): lax.ppermute(block, axis, [(i, i ^ bits) for i in range(lax.axis_size(axi...  200 us
    pallas_call x8, Pallas kernels, half_product(): pl.pallas_call(half_product_kernel, grid=(width // tile,), in_specs=[pl.B...  51 us
    ppermute x36, starting transfers between devices, swap(): lax.ppermute(block, axis, [(i, i ^ bits) for i in range(lax.axis_size(axi...  31.4 us
    pallas_call x2, Pallas kernels, assemble(): pl.pallas_call(functools.partial(assemble_kernel, blocks), grid_spec=pltp...  12 us
    dot_general x1, matrix products, merger(): jnp.dot(hidden, fc2_weight, preferred_element_type=jnp.float32)  9.75 us
    pallas_call x1, Pallas kernels, finish(): pl.pallas_call(functools.partial(finish_kernel, bounds, tiles), grid=(wid...  9.08 us
    unnamed x76, local copies, waits for them, and re-layouts  7.62 us
  transfers between devices with their start and end apart: 37, of which 15 were waited for; matrix products, arithmetic and copies ran while one was open for 10% of the time, Pallas kernels for 17%

profile of v1, /device:TPU:0, one launch (start us, length us, event | category | flops | bytes accessed | tf_op | source)
XLA Modules:
  0.0 361.4 jit_solution(1413801341938194651)
XLA Ops:
  26.7 9.8 %convolution_convert_fusion.2 = bf16[128,8192]{1,0:T(8,128)(2,1)S(1)} fusion(bf16[640,8192]{1,0:T(8,128)(2,1)} %param.19, bf16[5120,640]{1,0:T(8,128)(2,1)} %param.17, bf16[32,5120]{1,0:T(8,128)(2,1)} %collective-permute-done.2, bf16[32,5120]{1,0:T(8,128)(2,1)} %collective-permute-done.1, bf16[32,5120]{1,0:T(8,128)(2,1)} %collective-permute-done, ...), kind=kOutput, calls=%fused_computation.2 | convolution fusion | flops 2192736256 | bytes 20449792 | tf_op jit(solution)/shard_map/dot_general | solution.py:43
  38.8 12.1 %collective-permute-done.5 = bf16[32,8192]{1,0:T(8,128)(2,1)S(1)} collective-permute-done((bf16[32,8192]{1,0:T(8,128)(2,1)S(1)}, bf16[32,8192]{1,0:T(8,128)(2,1)S(1)}, u32[]{:S(2)}, u32[]{:S(2)}) %collective-permute-start.5) | collective-permute-done | bytes 524320 | tf_op jit(solution)/shard_map/ppermute | solution.py:34
  51.4 10.8 %collective-permute-done.4 = bf16[32,8192]{1,0:T(8,128)(2,1)S(1)} collective-permute-done((bf16[32,8192]{1,0:T(8,128)(2,1)S(1)}, bf16[32,8192]{1,0:T(8,128)(2,1)S(1)}, u32[]{:S(2)}, u32[]{:S(2)}) %collective-permute-start.4) | collective-permute-done | bytes 524320 | tf_op jit(solution)/shard_map/ppermute | solution.py:34
  75.8 52.1 %collective-permute-done.24.refs_2_ = bf16[1024,768]{1,0:T(8,128)(2,1)} collective-permute-done((bf16[1024,768]{1,0:T(8,128)(2,1)}, bf16[1024,768]{1,0:T(8,128)(2,1)}, u32[]{:S(2)}, u32[]{:S(2)}) %collective-permute-start.24) | collective-permute-done | bytes 1572896 | tf_op jit(solution)/shard_map/ppermute | solution.py:34
  136.2 18.1 %collective-permute-done.18.refs_2_ = bf16[128,4096]{1,0:T(8,128)(2,1)} collective-permute-done((bf16[128,4096]{1,0:T(8,128)(2,1)}, bf16[128,4096]{1,0:T(8,128)(2,1)}, u32[]{:S(2)}, u32[]{:S(2)}) %collective-permute-start.18) | collective-permute-done | bytes 1048608 | tf_op jit(solution)/shard_map/ppermute | solution.py:34
  154.8 11.5 %collective-permute-done.10.refs_4_.refs_8_ = bf16[32,4224]{1,0:T(8,128)(2,1)S(1)} collective-permute-done((bf16[32,4224]{1,0:T(8,128)(2,1)S(1)}, bf16[32,4224]{1,0:T(8,128)(2,1)S(1)}, u32[]{:S(2)}, u32[]{:S(2)}) %collective-permute-start.10) | collective-permute-done | bytes 270368 | tf_op jit(solution)/shard_map/ppermute | solution.py:34
  168.1 8.5 %collective-permute-done.8.refs_2_ = bf16[128,4096]{1,0:T(8,128)(2,1)S(1)} collective-permute-done((bf16[128,4096]{1,0:T(8,128)(2,1)}, bf16[128,4096]{1,0:T(8,128)(2,1)S(1)}, u32[]{:S(2)}, u32[]{:S(2)}) %collective-permute-start.8) | collective-permute-done | bytes 1048608 | tf_op jit(solution)/shard_map/ppermute | solution.py:34
  183.4 6.0 %assemble.2.tokens = bf16[512,4096]{1,0:T(8,128)(2,1)} custom-call(s32[1]{0:T(128)} %bitcast.place, bf16[128,4096]{1,0:T(8,128)(2,1)} %collective-permute-done.6.refs_0_, bf16[128,4096]{1,0:T(8,128)(2,1)} %copy-done.23, bf16[128,4096]{1,0:T(8,128)(2,1)} %copy-done.24, bf16[128,4096]{1,0:T(8,128)(2,1)} %copy-done.25, bf16[32,4224]{1,0:T(8,128)(2,1)} %copy-done.11, ...), custom_call_target="tpu_custom_call" | custom-call | bytes 8388608 | tf_op jit(solution)/shard_map/assemble/pallas_call | solution.py:116
  191.0 8.1 %shard_map.168 = bf16[512,768]{1,0:T(8,128)(2,1)} custom-call(bf16[512,4096]{1,0:T(8,128)(2,1)} %assemble.2.tokens, bf16[1024,768]{1,0:T(8,128)(2,1)} %get-tuple-element.42.refs_0_, bf16[1024,768]{1,0:T(8,128)(2,1)} %collective-permute-done.23.refs_1_, bf16[1024,768]{1,0:T(8,128)(2,1)} %collective-permute-done.24.refs_2_, ...), custom_call_target="tpu_custom_call" | custom-call | flops 3221225472 | bytes 10485760 | tf_op jit(solution)/shard_map/pallas_call | solution.py:172
  199.7 22.9 %collective-permute-done.30.refs_2_ = bf16[1024,512]{1,0:T(8,128)(2,1)} collective-permute-done((bf16[1024,512]{1,0:T(8,128)(2,1)S(1)}, bf16[1024,512]{1,0:T(8,128)(2,1)}, u32[]{:S(2)}, u32[]{:S(2)}) %collective-permute-start.30) | collective-permute-done | bytes 1048608 | tf_op jit(solution)/shard_map/ppermute | solution.py:34
  223.2 7.3 %shard_map.165 = bf16[512,768]{1,0:T(8,128)(2,1)S(1)} custom-call(bf16[512,4096]{1,0:T(8,128)(2,1)} %assemble.2.tokens, bf16[1024,768]{1,0:T(8,128)(2,1)} %get-tuple-element.43.refs_0_, bf16[1024,768]{1,0:T(8,128)(2,1)} %collective-permute-done.14.refs_1_, bf16[1024,768]{1,0:T(8,128)(2,1)} %collective-permute-done.15.refs_2_, ...), custom_call_target="tpu_custom_call" | custom-call | flops 3221225472 | bytes 10485760 | tf_op jit(solution)/shard_map/pallas_call | solution.py:172
  237.1 6.0 %assemble.3.tokens = bf16[512,4096]{1,0:T(8,128)(2,1)} custom-call(s32[1]{0:T(128)} %bitcast.place, bf16[128,4096]{1,0:T(8,128)(2,1)} %pad_maximum_fusion.refs_0_, bf16[128,4096]{1,0:T(8,128)(2,1)} %collective-permute-done.17.refs_1_, bf16[128,4096]{1,0:T(8,128)(2,1)} %collective-permute-done.18.refs_2_, bf16[128,4096]{1,0:T(8,128)(2,1)} %collective-permute-done.19.refs_3_, ...), custom_call_target="tpu_custom_call" | custom-call | bytes 8388608 | tf_op jit(solution)/shard_map/assemble/pallas_call | solution.py:116
  243.1 7.4 %shard_map.167.refs_1_ = f32[512,768]{1,0:T(8,128)S(1)} custom-call(bf16[512,4096]{1,0:T(8,128)(2,1)} %assemble.3.tokens, bf16[1024,768]{1,0:T(8,128)(2,1)} %get-tuple-element.43.refs_0_, bf16[1024,768]{1,0:T(8,128)(2,1)} %collective-permute-done.14.refs_1_, bf16[1024,768]{1,0:T(8,128)(2,1)} %collective-permute-done.15.refs_2_, ...), custom_call_target="tpu_custom_call" | custom-call | flops 3221225472 | bytes 10485760 | tf_op jit(solution)/shard_map/pallas_call | solution.py:172
  253.0 5.1 %shard_map.169 = bf16[512,512]{1,0:T(8,128)(2,1)S(1)} custom-call(bf16[512,4096]{1,0:T(8,128)(2,1)} %assemble.2.tokens, bf16[1024,512]{1,0:T(8,128)(2,1)S(1)} %get-tuple-element.28.refs_0_, bf16[1024,512]{1,0:T(8,128)(2,1)} %collective-permute-done.26.refs_1_, bf16[1024,512]{1,0:T(8,128)(2,1)S(1)} %collective-permute-done.27.refs_2_, ...), custom_call_target="tpu_custom_call" | custom-call | flops 2147483648 | bytes 8388608 | tf_op jit(solution)/shard_map/pallas_call | solution.py:172
  259.8 5.2 %shard_map.170.refs_2_ = f32[512,512]{1,0:T(8,128)S(1)} custom-call(bf16[512,4096]{1,0:T(8,128)(2,1)} %assemble.3.tokens, bf16[1024,512]{1,0:T(8,128)(2,1)S(1)} %get-tuple-element.28.refs_0_, bf16[1024,512]{1,0:T(8,128)(2,1)} %collective-permute-done.26.refs_1_, bf16[1024,512]{1,0:T(8,128)(2,1)S(1)} %collective-permute-done.27.refs_2_, ...), custom_call_target="tpu_custom_call" | custom-call | flops 2147483648 | bytes 8388608 | tf_op jit(solution)/shard_map/pallas_call | solution.py:172
  265.0 6.2 %collective-permute-done.29.refs_1_ = bf16[1024,512]{1,0:T(8,128)(2,1)} collective-permute-done((bf16[1024,512]{1,0:T(8,128)(2,1)S(1)}, bf16[1024,512]{1,0:T(8,128)(2,1)}, u32[]{:S(2)}, u32[]{:S(2)}) %collective-permute-start.29) | collective-permute-done | bytes 1048608 | tf_op jit(solution)/shard_map/ppermute | solution.py:34
  271.2 20.7 %collective-permute-done.31.refs_3_ = bf16[1024,512]{1,0:T(8,128)(2,1)} collective-permute-done((bf16[1024,512]{1,0:T(8,128)(2,1)}, bf16[1024,512]{1,0:T(8,128)(2,1)}, u32[]{:S(2)}, u32[]{:S(2)}) %collective-permute-start.31) | collective-permute-done | bytes 1048608 | tf_op jit(solution)/shard_map/ppermute | solution.py:34
  291.9 5.3 %shard_map.171 = bf16[512,512]{1,0:T(8,128)(2,1)S(1)} custom-call(bf16[512,4096]{1,0:T(8,128)(2,1)} %assemble.2.tokens, bf16[1024,512]{1,0:T(8,128)(2,1)S(1)} %get-tuple-element.32.refs_0_, bf16[1024,512]{1,0:T(8,128)(2,1)} %collective-permute-done.29.refs_1_, bf16[1024,512]{1,0:T(8,128)(2,1)} %collective-permute-done.30.refs_2_, ...), custom_call_target="tpu_custom_call" | custom-call | flops 2147483648 | bytes 8388608 | tf_op jit(solution)/shard_map/pallas_call | solution.py:172
  302.3 7.3 %shard_map.166.refs_0_ = f32[512,768]{1,0:T(8,128)S(1)} custom-call(bf16[512,4096]{1,0:T(8,128)(2,1)} %assemble.3.tokens, bf16[1024,768]{1,0:T(8,128)(2,1)} %get-tuple-element.42.refs_0_, bf16[1024,768]{1,0:T(8,128)(2,1)} %collective-permute-done.23.refs_1_, bf16[1024,768]{1,0:T(8,128)(2,1)} %collective-permute-done.24.refs_2_, ...), custom_call_target="tpu_custom_call" | custom-call | flops 3221225472 | bytes 10485760 | tf_op jit(solution)/shard_map/pallas_call | solution.py:172
  310.9 5.3 %shard_map.172.refs_3_ = f32[512,512]{1,0:T(8,128)S(1)} custom-call(bf16[512,4096]{1,0:T(8,128)(2,1)} %assemble.3.tokens, bf16[1024,512]{1,0:T(8,128)(2,1)S(1)} %get-tuple-element.32.refs_0_, bf16[1024,512]{1,0:T(8,128)(2,1)} %collective-permute-done.29.refs_1_, bf16[1024,512]{1,0:T(8,128)(2,1)} %collective-permute-done.30.refs_2_, ...), custom_call_target="tpu_custom_call" | custom-call | flops 2147483648 | bytes 8388608 | tf_op jit(solution)/shard_map/pallas_call | solution.py:172
  317.1 12.9 %collective-permute-done.33.refs_5_ = bf16[512,768]{1,0:T(8,128)(2,1)S(1)} collective-permute-done((bf16[512,768]{1,0:T(8,128)(2,1)S(1)}, bf16[512,768]{1,0:T(8,128)(2,1)S(1)}, u32[]{:S(2)}, u32[]{:S(2)}) %collective-permute-start.33) | collective-permute-done | bytes 786464 | tf_op jit(solution)/shard_map/ppermute | solution.py:34
  330.1 11.2 %collective-permute-done.34.refs_6_ = bf16[512,512]{1,0:T(8,128)(2,1)S(1)} collective-permute-done((bf16[512,512]{1,0:T(8,128)(2,1)S(1)}, bf16[512,512]{1,0:T(8,128)(2,1)S(1)}, u32[]{:S(2)}, u32[]{:S(2)}) %collective-permute-start.34) | collective-permute-done | bytes 524320 | tf_op jit(solution)/shard_map/ppermute | solution.py:34
  342.1 9.3 %collective-permute-done.35.refs_7_ = bf16[512,512]{1,0:T(8,128)(2,1)S(1)} collective-permute-done((bf16[512,512]{1,0:T(8,128)(2,1)S(1)}, bf16[512,512]{1,0:T(8,128)(2,1)S(1)}, u32[]{:S(2)}, u32[]{:S(2)}) %collective-permute-start.35) | collective-permute-done | bytes 524320 | tf_op jit(solution)/shard_map/ppermute | solution.py:34
  352.2 9.1 %finish.1 = (bf16[512,2048]{1,0:T(8,128)(2,1)}, bf16[512,256]{1,0:T(8,128)(2,1)}, bf16[512,256]{1,0:T(8,128)(2,1)}) custom-call(f32[1,2560]{1,0:T(1,128)} %broadcast_in_dim.12.bias_ref, f32[512,768]{1,0:T(8,128)} %copy-done.1, f32[512,768]{1,0:T(8,128)} %copy-done, f32[512,512]{1,0:T(8,128)} %copy-done.2, f32[512,512]{1,0:T(8,128)} %copy-done.3, ...), custom_call_target="tpu_custom_call" | custom-call | tf_op jit(solution)/shard_map/finish/pallas_call | solution.py:221
  (172 shorter events, 79.4 us)
Async XLA Ops:
  11.4 122.0 %collective-permute-start.14 = (bf16[1024,768]{1,0:T(8,128)(2,1)}, bf16[1024,768]{1,0:T(8,128)(2,1)}, u32[]{:S(2)}, u32[]{:S(2)}) collective-permute-start(bf16[1024,768]{1,0:T(8,128)(2,1)} %get-tuple-element.43.refs_0_), channel_id=1, source_target_pairs={{0,4},{4,0},{8,12},{12,8},{16,20},{20,16},{24,28},{28,24},{1,5},{5... | collective-permute-start | bytes 4718600 | tf_op jit(solution)/shard_map/ppermute | solution.py:34
  13.1 120.3 %collective-permute-start.15 = (bf16[1024,768]{1,0:T(8,128)(2,1)}, bf16[1024,768]{1,0:T(8,128)(2,1)}, u32[]{:S(2)}, u32[]{:S(2)}) collective-permute-start(bf16[1024,768]{1,0:T(8,128)(2,1)} %get-tuple-element.43.refs_0_), channel_id=1, source_target_pairs={{0,8},{4,12},{8,0},{12,4},{16,24},{20,28},{24,16},{28,20},{1,9},{5... | collective-permute-start | bytes 4718600 | tf_op jit(solution)/shard_map/ppermute | solution.py:34
  37.4 24.8 %collective-permute-start.4 = (bf16[32,8192]{1,0:T(8,128)(2,1)S(1)}, bf16[32,8192]{1,0:T(8,128)(2,1)S(1)}, u32[]{:S(2)}, u32[]{:S(2)}) collective-permute-start(bf16[32,8192]{1,0:T(8,128)(2,1)S(1)} %get-tuple-element.54), channel_id=1, source_target_pairs={{0,2},{1,3},{2,0},{3,1},{4,6},{5,7},{6,4},{7,5},{8,10},{9,11},{10,... | collective-permute-start | bytes 1572872 | tf_op jit(solution)/shard_map/ppermute | solution.py:34
  50.9 84.0 %collective-permute-start.23 = (bf16[1024,768]{1,0:T(8,128)(2,1)}, bf16[1024,768]{1,0:T(8,128)(2,1)}, u32[]{:S(2)}, u32[]{:S(2)}) collective-permute-start(bf16[1024,768]{1,0:T(8,128)(2,1)} %get-tuple-element.42.refs_0_), channel_id=1, source_target_pairs={{0,4},{4,0},{8,12},{12,8},{16,20},{20,16},{24,28},{28,24},{1,5},{5... | collective-permute-start | bytes 4718600 | tf_op jit(solution)/shard_map/ppermute | solution.py:34
  62.2 65.8 %collective-permute-start.24 = (bf16[1024,768]{1,0:T(8,128)(2,1)}, bf16[1024,768]{1,0:T(8,128)(2,1)}, u32[]{:S(2)}, u32[]{:S(2)}) collective-permute-start(bf16[1024,768]{1,0:T(8,128)(2,1)} %get-tuple-element.42.refs_0_), channel_id=1, source_target_pairs={{0,8},{4,12},{8,0},{12,4},{16,24},{20,28},{24,16},{28,20},{1,9},{5... | collective-permute-start | bytes 4718600 | tf_op jit(solution)/shard_map/ppermute | solution.py:34
  64.2 65.7 %all-to-all-start = ((bf16[8,4,8320]{2,1,0:T(4,128)(2,1)}), bf16[8,4,8320]{2,1,0:T(4,128)(2,1)S(1)}, u32[]{:S(2)}, u32[]{:S(2)}) async-start(bf16[8,4,8320]{2,1,0:T(4,128)(2,1)} %reshape.57), calls=%async_computation | async-start | bytes 1064960 | tf_op jit(solution)/shard_map/all_to_all | solution.py:296
  70.2 63.1 %collective-permute-start.6 = (bf16[128,4096]{1,0:T(8,128)(2,1)}, bf16[128,4096]{1,0:T(8,128)(2,1)}, u32[]{:S(2)}, u32[]{:S(2)}) collective-permute-start(bf16[128,4096]{1,0:T(8,128)(2,1)} %pad_maximum_fusion.1), channel_id=1, source_target_pairs={{0,16},{4,20},{8,24},{12,28},{16,0},{20,4},{24,8},{28,12},{1,17},{... | collective-permute-start | bytes 3145736 | tf_op jit(solution)/shard_map/ppermute | solution.py:34
  127.9 26.3 %collective-permute-start.18 = (bf16[128,4096]{1,0:T(8,128)(2,1)}, bf16[128,4096]{1,0:T(8,128)(2,1)}, u32[]{:S(2)}, u32[]{:S(2)}) collective-permute-start(bf16[128,4096]{1,0:T(8,128)(2,1)} %pad_maximum_fusion.refs_0_), channel_id=1, source_target_pairs={{0,2},{1,3},{2,0},{3,1},{4,6},{5,7},{6,4},{7,5},{8,10},{9,11},{10,... | collective-permute-start | bytes 3145736 | tf_op jit(solution)/shard_map/ppermute | solution.py:34
  133.2 34.9 %collective-permute-start.27 = (bf16[1024,512]{1,0:T(8,128)(2,1)S(1)}, bf16[1024,512]{1,0:T(8,128)(2,1)S(1)}, u32[]{:S(2)}, u32[]{:S(2)}) collective-permute-start(bf16[1024,512]{1,0:T(8,128)(2,1)S(1)} %get-tuple-element.28.refs_0_), channel_id=1, source_target_pairs={{0,8},{4,12},{8,0},{12,4},{16,24},{20,28},{24,16},{28,20},{1,9},{5... | collective-permute-start | bytes 3145736 | tf_op jit(solution)/shard_map/ppermute | solution.py:34
  133.4 43.3 %collective-permute-start.7 = (bf16[128,4096]{1,0:T(8,128)(2,1)}, bf16[128,4096]{1,0:T(8,128)(2,1)S(1)}, u32[]{:S(2)}, u32[]{:S(2)}) collective-permute-start(bf16[128,4096]{1,0:T(8,128)(2,1)} %collective-permute-done.6.refs_0_), channel_id=1, source_target_pairs={{0,1},{1,0},{2,3},{3,2},{4,5},{5,4},{6,7},{7,6},{8,9},{9,8},{10,11... | collective-permute-start | bytes 3145736 | tf_op jit(solution)/shard_map/ppermute | solution.py:34
  133.5 43.2 %collective-permute-start.8 = (bf16[128,4096]{1,0:T(8,128)(2,1)}, bf16[128,4096]{1,0:T(8,128)(2,1)S(1)}, u32[]{:S(2)}, u32[]{:S(2)}) collective-permute-start(bf16[128,4096]{1,0:T(8,128)(2,1)} %collective-permute-done.6.refs_0_), channel_id=1, source_target_pairs={{0,2},{1,3},{2,0},{3,1},{4,6},{5,7},{6,4},{7,5},{8,10},{9,11},{10,... | collective-permute-start | bytes 3145736 | tf_op jit(solution)/shard_map/ppermute | solution.py:34
  134.9 54.5 %collective-permute-start.25 = (bf16[1024,768]{1,0:T(8,128)(2,1)}, bf16[1024,768]{1,0:T(8,128)(2,1)}, u32[]{:S(2)}, u32[]{:S(2)}) collective-permute-start(bf16[1024,768]{1,0:T(8,128)(2,1)} %collective-permute-done.24.refs_2_), channel_id=1, source_target_pairs={{0,4},{4,0},{8,12},{12,8},{16,20},{20,16},{24,28},{28,24},{1,5},{5... | collective-permute-start | bytes 4718600 | tf_op jit(solution)/shard_map/ppermute | solution.py:34
  168.1 54.5 %collective-permute-start.16 = (bf16[1024,768]{1,0:T(8,128)(2,1)}, bf16[1024,768]{1,0:T(8,128)(2,1)}, u32[]{:S(2)}, u32[]{:S(2)}) collective-permute-start(bf16[1024,768]{1,0:T(8,128)(2,1)} %collective-permute-done.14.refs_1_), channel_id=1, source_target_pairs={{0,8},{4,12},{8,0},{12,4},{16,24},{20,28},{24,16},{28,20},{1,9},{5... | collective-permute-start | bytes 4718600 | tf_op jit(solution)/shard_map/ppermute | solution.py:34
  181.5 41.0 %collective-permute-start.30 = (bf16[1024,512]{1,0:T(8,128)(2,1)S(1)}, bf16[1024,512]{1,0:T(8,128)(2,1)}, u32[]{:S(2)}, u32[]{:S(2)}) collective-permute-start(bf16[1024,512]{1,0:T(8,128)(2,1)S(1)} %get-tuple-element.32.refs_0_), channel_id=1, source_target_pairs={{0,8},{4,12},{8,0},{12,4},{16,24},{20,28},{24,16},{28,20},{1,9},{5... | collective-permute-start | bytes 3145736 | tf_op jit(solution)/shard_map/ppermute | solution.py:34
  183.2 52.2 %collective-permute-start.19 = (bf16[128,4096]{1,0:T(8,128)(2,1)}, bf16[128,4096]{1,0:T(8,128)(2,1)}, u32[]{:S(2)}, u32[]{:S(2)}) collective-permute-start(bf16[128,4096]{1,0:T(8,128)(2,1)} %collective-permute-done.18.refs_2_), channel_id=1, source_target_pairs={{0,1},{1,0},{2,3},{3,2},{4,5},{5,4},{6,7},{7,6},{8,9},{9,8},{10,11... | collective-permute-start | bytes 3145736 | tf_op jit(solution)/shard_map/ppermute | solution.py:34
  189.4 33.2 %collective-permute-start.21 = (bf16[32,4224]{1,0:T(8,128)(2,1)S(1)}, bf16[32,4224]{1,0:T(8,128)(2,1)S(1)}, u32[]{:S(2)}, u32[]{:S(2)}) collective-permute-start(bf16[32,4224]{1,0:T(8,128)(2,1)S(1)} %get-tuple-element.55.refs_4_.refs_8_), channel_id=1, source_target_pairs={{0,2},{1,3},{2,0},{3,1},{4,6},{5,7},{6,4},{7,5},{8,10},{9,11},{10,... | collective-permute-start | bytes 811016 | tf_op jit(solution)/shard_map/ppermute | solution.py:34
  199.1 52.6 %collective-permute-start.26 = (bf16[1024,512]{1,0:T(8,128)(2,1)S(1)}, bf16[1024,512]{1,0:T(8,128)(2,1)}, u32[]{:S(2)}, u32[]{:S(2)}) collective-permute-start(bf16[1024,512]{1,0:T(8,128)(2,1)S(1)} %get-tuple-element.28.refs_0_), channel_id=1, source_target_pairs={{0,4},{4,0},{8,12},{12,8},{16,20},{20,16},{24,28},{28,24},{1,5},{5... | collective-permute-start | bytes 3145736 | tf_op jit(solution)/shard_map/ppermute | solution.py:34
  222.6 30.5 %collective-permute-start.28 = (bf16[1024,512]{1,0:T(8,128)(2,1)S(1)}, bf16[1024,512]{1,0:T(8,128)(2,1)}, u32[]{:S(2)}, u32[]{:S(2)}) collective-permute-start(bf16[1024,512]{1,0:T(8,128)(2,1)S(1)} %collective-permute-done.27.refs_2_), channel_id=1, source_target_pairs={{0,4},{4,0},{8,12},{12,8},{16,20},{20,16},{24,28},{28,24},{1,5},{5... | collective-permute-start | bytes 3145736 | tf_op jit(solution)/shard_map/ppermute | solution.py:34
  231.4 39.8 %collective-permute-start.29 = (bf16[1024,512]{1,0:T(8,128)(2,1)S(1)}, bf16[1024,512]{1,0:T(8,128)(2,1)}, u32[]{:S(2)}, u32[]{:S(2)}) collective-permute-start(bf16[1024,512]{1,0:T(8,128)(2,1)S(1)} %get-tuple-element.32.refs_0_), channel_id=1, source_target_pairs={{0,4},{4,0},{8,12},{12,8},{16,20},{20,16},{24,28},{28,24},{1,5},{5... | collective-permute-start | bytes 3145736 | tf_op jit(solution)/shard_map/ppermute | solution.py:34
  233.4 58.5 %collective-permute-start.31 = (bf16[1024,512]{1,0:T(8,128)(2,1)}, bf16[1024,512]{1,0:T(8,128)(2,1)}, u32[]{:S(2)}, u32[]{:S(2)}) collective-permute-start(bf16[1024,512]{1,0:T(8,128)(2,1)} %collective-permute-done.30.refs_2_), channel_id=1, source_target_pairs={{0,4},{4,0},{8,12},{12,8},{16,20},{20,16},{24,28},{28,24},{1,5},{5... | collective-permute-start | bytes 3145736 | tf_op jit(solution)/shard_map/ppermute | solution.py:34
  235.5 81.7 %collective-permute-start.32 = (bf16[512,768]{1,0:T(8,128)(2,1)}, bf16[512,768]{1,0:T(8,128)(2,1)}, u32[]{:S(2)}, u32[]{:S(2)}) collective-permute-start(bf16[512,768]{1,0:T(8,128)(2,1)} %shard_map.168), channel_id=1, source_target_pairs={{0,16},{4,20},{8,24},{12,28},{16,0},{20,4},{24,8},{28,12},{1,17},{... | collective-permute-start | bytes 2359304 | tf_op jit(solution)/shard_map/ppermute | solution.py:34
  251.7 78.4 %collective-permute-start.33 = (bf16[512,768]{1,0:T(8,128)(2,1)S(1)}, bf16[512,768]{1,0:T(8,128)(2,1)S(1)}, u32[]{:S(2)}, u32[]{:S(2)}) collective-permute-start(bf16[512,768]{1,0:T(8,128)(2,1)S(1)} %copy-done.5), channel_id=1, source_target_pairs={{0,16},{4,20},{8,24},{12,28},{16,0},{20,4},{24,8},{28,12},{1,17},{... | collective-permute-start | bytes 2359304 | tf_op jit(solution)/shard_map/ppermute | solution.py:34
  258.1 83.2 %collective-permute-start.34 = (bf16[512,512]{1,0:T(8,128)(2,1)S(1)}, bf16[512,512]{1,0:T(8,128)(2,1)S(1)}, u32[]{:S(2)}, u32[]{:S(2)}) collective-permute-start(bf16[512,512]{1,0:T(8,128)(2,1)S(1)} %shard_map.169), channel_id=1, source_target_pairs={{0,16},{4,20},{8,24},{12,28},{16,0},{20,4},{24,8},{28,12},{1,17},{... | collective-permute-start | bytes 1572872 | tf_op jit(solution)/shard_map/ppermute | solution.py:34
  297.2 54.2 %collective-permute-start.35 = (bf16[512,512]{1,0:T(8,128)(2,1)S(1)}, bf16[512,512]{1,0:T(8,128)(2,1)S(1)}, u32[]{:S(2)}, u32[]{:S(2)}) collective-permute-start(bf16[512,512]{1,0:T(8,128)(2,1)S(1)} %shard_map.171), channel_id=1, source_target_pairs={{0,16},{4,20},{8,24},{12,28},{16,0},{20,4},{24,8},{28,12},{1,17},{... | collective-permute-start | bytes 1572872 | tf_op jit(solution)/shard_map/ppermute | solution.py:34
  (49 other events, 591.7 us)
